TPU v7x, 32 devices: a whole 2x2x4 slice. The times are simulated.
32 devices in a mesh: line: 2 (over x), track: 16 (over z, y, core).
Axes of the slice: x: 2, y: 2, z: 4, core: 2. Of those that a mesh axis runs over, the one named last changes fastest.
Arguments:
- radiance: bfloat16 [2, 64, 224, 1000], P('line', 'track'), may hold values from -40 to 40, as said below
Outputs:
- cleaned: bfloat16 [2, 64, 224, 1000], P('line', 'track')
- filter_matrix: float32 [224, 224], replicated
Inputs may be any that keep to these rules, and one draw needn't show every extreme that they name: `radiance`: every flightline, band and column carries a column offset, a column gain and pixel noise, so no column is constant along track.
All inputs are finite; a program needn't handle non-finite values.
Results may differ from a plain program's by a relative error of at most 0.0045.
Values may be sent and summed in bfloat16 or wider, within the bound.
A program may use at most 64 MiB of HBM per device.

v0:
```python
import jax
import jax.numpy as jnp
from jax import lax
from jax.sharding import PartitionSpec as P

NCOMP = 40
ITERS = 4
EPSILON = 1e-05
HIGHEST = lax.Precision.HIGHEST


def from_behind(block, axis, distance):
    devices = range(lax.axis_size(axis))
    route = [(i - distance, i) for i in devices if i - distance in devices]
    return lax.ppermute(block, axis, route)


def column_terms(first_total, second_total, total_rows):
    col_mean = first_total / total_rows
    col_spread = jnp.sqrt(second_total / total_rows - col_mean * col_mean + EPSILON)
    band_mean = jnp.mean(col_mean, axis=1)
    factor = jnp.mean(col_spread, axis=1)[:, None] / col_spread
    return (col_mean, factor, band_mean)


def pick_entry(vector, position, places):
    return jnp.sum(jnp.where(places == position, vector, 0.0))


def lower_factor(matrix):
    size = matrix.shape[0]
    places = jnp.arange(size)

    def one_column(column_id, factor):
        factor_row = lax.dynamic_slice_in_dim(factor, column_id, 1, 0)[0]
        column = lax.dynamic_slice_in_dim(matrix, column_id, 1, 1)[:, 0] - jnp.dot(
            factor, factor_row, precision=HIGHEST
        )
        pivot = jnp.sqrt(pick_entry(column, column_id, places))
        entries = jnp.where(places == column_id, pivot, column / pivot)
        entries = jnp.where(places >= column_id, entries, 0.0)
        return jnp.where(places[None, :] == column_id, entries[:, None], factor)

    return lax.fori_loop(0, size, one_column, jnp.zeros_like(matrix))


def lower_solve(factor, right_side):
    size = factor.shape[0]
    places = jnp.arange(size)

    def one_row(row_id, solved):
        factor_row = lax.dynamic_slice_in_dim(factor, row_id, 1, 0)[0]
        target = lax.dynamic_slice_in_dim(right_side, row_id, 1, 0)[0]
        pivot = pick_entry(factor_row, row_id, places)
        entries = (target - jnp.dot(factor_row, solved, precision=HIGHEST)) / pivot
        return lax.dynamic_update_slice_in_dim(solved, entries[None], row_id, 0)

    return lax.fori_loop(0, size, one_row, jnp.zeros_like(right_side))


def upper_solve(factor, right_side):
    flipped = factor.T[::-1, ::-1]
    return lower_solve(flipped, right_side[::-1])[::-1]


def mnf_filter(signal_gram, noise_gram, kept):
    noise_factor = lower_factor(noise_gram)
    half_solved = lower_solve(noise_factor, signal_gram)
    whitened = lower_solve(noise_factor, half_solved.T)
    whitened = 0.5 * (whitened + whitened.T)
    subspace = jnp.eye(whitened.shape[0], kept, dtype=jnp.float32)
    for iteration in range(ITERS):
        mapped = jnp.dot(whitened, subspace, precision=HIGHEST)
        inner_gram = jnp.dot(mapped.T, mapped, precision=HIGHEST)
        inner_factor = lower_factor(inner_gram)
        subspace = lower_solve(inner_factor, mapped.T).T
    forward_map = upper_solve(noise_factor, subspace)
    backward_map = jnp.dot(noise_factor, subspace, precision=HIGHEST)
    return jnp.dot(forward_map, backward_map.T, precision=HIGHEST)


def body(radiance):
    local_block = radiance[0]
    row_count = local_block.shape[0]
    column_count = local_block.shape[2]
    track_count = lax.axis_size("track")
    line_count = lax.axis_size("line")
    total_rows = row_count * track_count
    values = local_block.astype(jnp.float32)
    first_sum = jnp.sum(values, axis=0)
    second_sum = jnp.sum(values * values, axis=0)
    first_total, second_total = lax.psum((first_sum, second_sum), "track")
    col_mean, factor, band_mean = column_terms(first_total, second_total, total_rows)
    centred = ((values - col_mean) * factor).astype(jnp.bfloat16)
    following = from_behind(centred[:1], "track", -1)
    rows_ahead = jnp.concatenate([centred[1:], following], axis=0)
    keep_last = lax.axis_index("track") < track_count - 1
    row_index = jnp.arange(row_count)
    row_keep = jnp.where((row_index < row_count - 1) | keep_last, 1.0, 0.0).astype(jnp.float32)
    differences = (
        (rows_ahead.astype(jnp.float32) - centred.astype(jnp.float32)) * row_keep[:, None, None]
    ).astype(jnp.bfloat16)
    signal_part = jnp.einsum("rbc,rdc->bd", centred, centred, preferred_element_type=jnp.float32)
    noise_part = jnp.einsum(
        "rbc,rdc->bd", differences, differences, preferred_element_type=jnp.float32
    )
    signal_total, noise_total = lax.psum((signal_part, noise_part), ("line", "track"))
    signal_gram = signal_total / (line_count * total_rows * column_count)
    noise_gram = noise_total / (2 * line_count * (total_rows - 1) * column_count)
    filter_matrix = mnf_filter(signal_gram, noise_gram, NCOMP)
    narrow = filter_matrix.astype(jnp.bfloat16)
    mixed = jnp.einsum("ab,rac->rbc", narrow, centred, preferred_element_type=jnp.float32)
    cleaned = (band_mean[:, None] + mixed).astype(jnp.bfloat16)
    return (cleaned[None], filter_matrix)


def solution(mesh):
    in_specs = (P("line", "track", None, None),)
    out_specs = (P("line", "track", None, None), P())
    return jax.shard_map(body, mesh=mesh, in_specs=in_specs, out_specs=out_specs, check_vma=False)
```

profile of v0, /device:TPU:1, one launch (start us, length us, event | category | flops | bytes accessed | tf_op | source)
XLA Modules:
  0.0 2186.4 jit_solution(16834112207716151684)
XLA Ops:
  7.2 3.0 convert_reduce_fusion
  10.2 1.3 fusion.71
  11.6 98.9 %all-reduce.7.cloned.1.call-done = (f32[224,1000]{1,0:T(8,128)}, f32[224,1000]{1,0:T(8,128)}) async-done(((f32[224,1000]{1,0:T(8,128)}, f32[224,1000]{1,0:T(8,128)}), (f32[224,1000]{1,0:T(8,128)}, f32[224,1000]{1,0:T(8,128)})) %all-reduce.7.cloned.1.call-update) | async-done | bytes 1792016 | tf_op jit(solution)/shard_map/psum | solution.py:92
  110.5 2.2 fusion.85
  113.2 1.0 copy-done.1
  114.9 3.6 collective-permute-start
  118.6 1.4 convolution_bitcast_fusion.5
  120.0 5.5 collective-permute-done
  125.5 2.0 fusion.78
  127.5 127.6 %all-reduce.5.cloned.1.call-done = (f32[224,224]{1,0:T(8,128)}, f32[224,224]{1,0:T(8,128)}) async-done(((f32[224,224]{1,0:T(8,128)}, f32[224,224]{1,0:T(8,128)}), (f32[224,224]{1,0:T(8,128)}, f32[224,224]{1,0:T(8,128)})) %all-reduce.5.cloned.1.call-update) | async-done | bytes 401424 | tf_op jit(solution)/shard_map/psum | solution.py:107
  255.1 1.1 broadcast_multiply_fusion.1
  256.3 401.2 %while.180 = (s32[]{:T(128)}, f32[224,224]{1,0:T(8,128)S(1)}, f32[224,224]{0,1:T(8,128)S(1)}, s32[]{:T(128)}, s32[]{:T(128)}) while((s32[]{:T(128)}, f32[224,224]{1,0:T(8,128)S(1)}, f32[224,224]{0,1:T(8,128)S(1)}, s32[]{:T(128)}, s32[]{:T(128)}) %tuple.370), condition=%wide.region_9.10_spmd.clone.clone, body=%wide.region_7.0_spmd.clone.clone.sunk | while | flops 754882 | bytes 1041836 | solution.py:44
  657.5 346.7 %while.173 = (s32[]{:T(128)}, f32[224,224]{1,0:T(8,128)S(1)}, f32[224,224]{1,0:T(8,128)S(1)}, f32[224,224]{1,0:T(8,128)S(1)}, s32[]{:T(128)}, /*index=5*/s32[]{:T(128)}) while((s32[]{:T(128)}, f32[224,224]{1,0:T(8,128)S(1)}, f32[224,224]{1,0:T(8,128)S(1)}, f32[224,224]{1,0:T(8,128)S(1)}, s32[]{:T(128)}, ...), condition=%wide.region_13.14_spmd.clone, body=%wide.region_11.13_spmd.clone.sunk | while | flops 603233 | bytes 211545 | solution.py:58
  1004.4 346.7 %while.174 = (s32[]{:T(128)}, f32[224,224]{1,0:T(8,128)S(1)}, f32[224,224]{1,0:T(8,128)S(1)}, f32[224,224]{1,0:T(8,128)S(1)}, s32[]{:T(128)}, /*index=5*/s32[]{:T(128)}) while((s32[]{:T(128)}, f32[224,224]{1,0:T(8,128)S(1)}, f32[224,224]{1,0:T(8,128)S(1)}, f32[224,224]{1,0:T(8,128)S(1)}, s32[]{:T(128)}, ...), condition=%wide.region_16.17_spmd.clone, body=%wide.region_14.16_spmd.clone.sunk | while | flops 603233 | bytes 211545 | solution.py:58
  1351.8 62.4 %while.181 = (s32[]{:T(128)}, f32[40,40]{1,0:T(8,128)S(1)}, f32[40,40]{0,1:T(8,128)S(1)}, s32[]{:T(128)}, s32[]{:T(128)}) while((s32[]{:T(128)}, f32[40,40]{1,0:T(8,128)S(1)}, f32[40,40]{0,1:T(8,128)S(1)}, s32[]{:T(128)}, s32[]{:T(128)}) %tuple.379), condition=%wide.region_19.20_spmd.clone.clone, body=%wide.region_17.19_spmd.clone.clone.sunk | while | flops 24402 | bytes 49456 | solution.py:44
  1414.2 58.8 %while.175 = (s32[]{:T(128)}, f32[40,224]{1,0:T(8,128)S(1)}, f32[40,224]{1,0:T(8,128)S(1)}, f32[40,40]{1,0:T(8,128)S(1)}, s32[]{:T(128)}, /*index=5*/s32[]{:T(128)}) while((s32[]{:T(128)}, f32[40,224]{1,0:T(8,128)S(1)}, f32[40,224]{1,0:T(8,128)S(1)}, f32[40,40]{1,0:T(8,128)S(1)}, s32[]{:T(128)}, /*index=5*/s32[]{:T(128)}) %tuple.416), condition=%wide.region_22.23_spmd.clone, body=%wide.region_20.22_spmd.clone.sunk | while | flops 108089 | bytes 49913 | solution.py:58
  1473.5 62.4 %while.182 = (s32[]{:T(128)}, f32[40,40]{1,0:T(8,128)S(1)}, f32[40,40]{0,1:T(8,128)S(1)}, s32[]{:T(128)}, s32[]{:T(128)}) while((s32[]{:T(128)}, f32[40,40]{1,0:T(8,128)S(1)}, f32[40,40]{0,1:T(8,128)S(1)}, s32[]{:T(128)}, s32[]{:T(128)}) %tuple.385), condition=%wide.region_25.26_spmd.clone.clone, body=%wide.region_23.25_spmd.clone.clone.sunk | while | flops 24402 | bytes 49456 | solution.py:44
  1535.9 58.8 %while.176 = (s32[]{:T(128)}, f32[40,224]{1,0:T(8,128)S(1)}, f32[40,224]{1,0:T(8,128)S(1)}, f32[40,40]{1,0:T(8,128)S(1)}, s32[]{:T(128)}, /*index=5*/s32[]{:T(128)}) while((s32[]{:T(128)}, f32[40,224]{1,0:T(8,128)S(1)}, f32[40,224]{1,0:T(8,128)S(1)}, f32[40,40]{1,0:T(8,128)S(1)}, s32[]{:T(128)}, /*index=5*/s32[]{:T(128)}) %tuple.414), condition=%wide.region_28.29_spmd.clone, body=%wide.region_26.28_spmd.clone.sunk | while | flops 108089 | bytes 49913 | solution.py:58
  1595.2 62.4 %while.183 = (s32[]{:T(128)}, f32[40,40]{1,0:T(8,128)S(1)}, f32[40,40]{0,1:T(8,128)S(1)}, s32[]{:T(128)}, s32[]{:T(128)}) while((s32[]{:T(128)}, f32[40,40]{1,0:T(8,128)S(1)}, f32[40,40]{0,1:T(8,128)S(1)}, s32[]{:T(128)}, s32[]{:T(128)}) %tuple.391), condition=%wide.region_31.32_spmd.clone.clone, body=%wide.region_29.31_spmd.clone.clone.sunk | while | flops 24402 | bytes 49456 | solution.py:44
  1657.6 58.8 %while.177 = (s32[]{:T(128)}, f32[40,224]{1,0:T(8,128)S(1)}, f32[40,224]{1,0:T(8,128)S(1)}, f32[40,40]{1,0:T(8,128)S(1)}, s32[]{:T(128)}, /*index=5*/s32[]{:T(128)}) while((s32[]{:T(128)}, f32[40,224]{1,0:T(8,128)S(1)}, f32[40,224]{1,0:T(8,128)S(1)}, f32[40,40]{1,0:T(8,128)S(1)}, s32[]{:T(128)}, /*index=5*/s32[]{:T(128)}) %tuple.415), condition=%wide.region_34.35_spmd.clone, body=%wide.region_32.34_spmd.clone.sunk | while | flops 108089 | bytes 49913 | solution.py:58
  1716.9 62.4 %while.184 = (s32[]{:T(128)}, f32[40,40]{1,0:T(8,128)S(1)}, f32[40,40]{0,1:T(8,128)S(1)}, s32[]{:T(128)}, s32[]{:T(128)}) while((s32[]{:T(128)}, f32[40,40]{1,0:T(8,128)S(1)}, f32[40,40]{0,1:T(8,128)S(1)}, s32[]{:T(128)}, s32[]{:T(128)}) %tuple.397), condition=%wide.region_37.38_spmd.clone.clone, body=%wide.region_35.37_spmd.clone.clone.sunk | while | flops 24402 | bytes 49456 | solution.py:44
  1779.3 58.8 %while.178 = (s32[]{:T(128)}, f32[40,224]{1,0:T(8,128)S(1)}, f32[40,224]{1,0:T(8,128)S(1)}, f32[40,40]{1,0:T(8,128)S(1)}, s32[]{:T(128)}, /*index=5*/s32[]{:T(128)}) while((s32[]{:T(128)}, f32[40,224]{1,0:T(8,128)S(1)}, f32[40,224]{1,0:T(8,128)S(1)}, f32[40,40]{1,0:T(8,128)S(1)}, s32[]{:T(128)}, /*index=5*/s32[]{:T(128)}) %tuple.413), condition=%wide.region_40.41_spmd.clone, body=%wide.region_38.40_spmd.clone.sunk | while | flops 108089 | bytes 49913 | solution.py:58
  1839.8 336.9 %while.179 = (s32[]{:T(128)}, f32[224,40]{1,0:T(8,128)S(1)}, f32[224,40]{1,0:T(8,128)S(1)}, f32[224,224]{1,0:T(8,128)S(1)}, s32[]{:T(128)}, /*index=5*/s32[]{:T(128)}) while((s32[]{:T(128)}, f32[224,40]{1,0:T(8,128)S(1)}, f32[224,40]{1,0:T(8,128)S(1)}, f32[224,224]{1,0:T(8,128)S(1)}, s32[]{:T(128)}, /*index=5*/s32[]{:T(128)}) %tuple.403), condition=%wide.region_43.44_spmd.clone, body=%wide.region_41.43_spmd.clone.sunk | while | flops 108273 | bytes 121013 | solution.py:58
  1842.0 0.8 fusion.191
  1843.5 0.8 fusion.191
  1845.0 0.8 fusion.191
  1846.5 0.8 fusion.191
  1849.5 0.8 fusion.191
  1852.5 0.8 fusion.191
  1855.5 0.8 fusion.191
  1858.5 0.8 fusion.191
  1861.5 0.8 fusion.191
  1864.5 0.8 fusion.191
  1867.5 0.8 fusion.191
  1870.5 0.8 fusion.191
  1872.0 0.8 fusion.191
  1873.6 0.8 fusion.191
  1875.1 0.8 fusion.191
  1878.1 0.8 fusion.191
  1881.1 0.8 fusion.191
  1884.1 0.8 fusion.191
  1887.1 0.8 fusion.191
  1890.1 0.8 fusion.191
  1893.1 0.8 fusion.191
  1896.1 0.8 fusion.191
  1899.1 0.8 fusion.191
  1900.6 0.8 fusion.191
  2177.4 2.1 fusion.77
  (6332 shorter events, 1593.9 us)
Async XLA Ops:
  7.2 3.0 copy-start
  7.2 103.3 %all-reduce.7.cloned.1.call-start = ((), (), s32[]{:S(2)}) async-start(), calls=%async_computation.1 | async-start | bytes 3670016 | tf_op jit(solution)/shard_map/psum | solution.py:92
  11.5 243.6 %all-reduce.5.cloned.1.call-start = ((), (), s32[]{:S(2)}) async-start(), calls=%async_computation | async-start | bytes 917504 | tf_op jit(solution)/shard_map/psum | solution.py:107
  110.5 2.3 copy-start.2
  110.5 2.3 copy-start.3
  112.8 1.5 copy-start.1
  114.9 10.6 collective-permute-start
  2177.4 2.1 copy-start.4
Sparse Core Ops, SparseCore 0:
  12.1 98.3 all-reduce.6
  127.6 127.4 all-reduce.4
where the time goes:
time: 2200 us; the launch traced here: 2190 us
  other arithmetic  1100 us (50%)
  matrix products  467 us (21%)
  loops' own time  309 us (14%)
  waiting for transfers between devices  232 us (11%)
  local copies, waits for them, and re-layouts  62 us (3%)
    reduce_sum x1056, other arithmetic, pick_entry(): return jnp.sum(jnp.where(places == position, vector, 0.0))  636 us
    div x608, other arithmetic, one_row(): entries = (target - jnp.dot(factor_row, solved, precision=HIGHEST)) / pivot  409 us
    dot_general x832, matrix products, one_row(): entries = (target - jnp.dot(factor_row, solved, precision=HIGHEST)) / pivot  285 us
    another operation x5, loops' own time, lower_factor(): return lax.fori_loop(0, size, one_column, jnp.zeros_like(matrix))  281 us
    dot_general x384, matrix products, one_column(): jnp.dot(factor, factor_row, precision=HIGHEST)  174 us
    psum x1, waiting for transfers between devices, body(): lax.psum((signal_part, noise_part), ('line', 'track'))  128 us
    psum x1, waiting for transfers between devices, body(): first_total, second_total = lax.psum((first_sum, second_sum), 'track')  98.9 us

commit v1 on v0

--- a/solution.py
+++ b/solution.py
@@ -104,7 +104,7 @@
     noise_part = jnp.einsum(
         "rbc,rdc->bd", differences, differences, preferred_element_type=jnp.float32
     )
-    signal_total, noise_total = lax.psum((signal_part, noise_part), ("line", "track"))
+    signal_total, noise_total = lax.psum(lax.psum((signal_part, noise_part), "track"), "line")
     signal_gram = signal_total / (line_count * total_rows * column_count)
     noise_gram = noise_total / (2 * line_count * (total_rows - 1) * column_count)
     filter_matrix = mnf_filter(signal_gram, noise_gram, NCOMP)

time: 2200 us -> 2310 us (1.050)
  other arithmetic: 1100 us -> 1190 us
    reduce_sum x1056, other arithmetic: 636 us -> 702 us  [pick_entry(): return jnp.sum(jnp.where(places == position, vector, 0.0))]
    div x608, other arithmetic: 409 us -> 435 us  [one_row(): entries = (target - jnp.dot(factor_row, solved, precision=HIGHEST)) / pivot]
    psum x1 -> x2, waiting for transfers between devices: 128 us -> 119 us  [the longest x1 89.8 us: body(): lax.psum((signal_part, noise_part), 'track')]
where the time goes in v1:
time: 2310 us; the launch traced here: 2300 us
  other arithmetic  1190 us (52%)
  matrix products  480 us (21%)
  loops' own time  325 us (14%)
  waiting for transfers between devices  224 us (10%)
  local copies, waits for them, and re-layouts  62 us (3%)
    reduce_sum x1056, other arithmetic, pick_entry(): return jnp.sum(jnp.where(places == position, vector, 0.0))  702 us
    div x608, other arithmetic, one_row(): entries = (target - jnp.dot(factor_row, solved, precision=HIGHEST)) / pivot  435 us
    another operation x5, loops' own time, lower_factor(): return lax.fori_loop(0, size, one_column, jnp.zeros_like(matrix))  298 us
    dot_general x832, matrix products, one_row(): entries = (target - jnp.dot(factor_row, solved, precision=HIGHEST)) / pivot  285 us
    dot_general x384, matrix products, one_column(): jnp.dot(factor, factor_row, precision=HIGHEST)  187 us
    psum x1, waiting for transfers between devices, body(): first_total, second_total = lax.psum((first_sum, second_sum), 'track')  98.9 us
    psum x1, waiting for transfers between devices, body(): lax.psum((signal_part, noise_part), 'track')  89.8 us

profile of v1, /device:TPU:1, one launch (start us, length us, event | category | flops | bytes accessed | tf_op | source)
XLA Modules:
  0.0 2300.3 jit_solution(2530197120994814131)
XLA Ops:
  7.2 3.0 convert_reduce_fusion
  10.2 1.3 fusion.71
  11.6 98.9 %all-reduce.9.cloned.1.call-done = (f32[224,1000]{1,0:T(8,128)}, f32[224,1000]{1,0:T(8,128)}) async-done(((f32[224,1000]{1,0:T(8,128)}, f32[224,1000]{1,0:T(8,128)}), (f32[224,1000]{1,0:T(8,128)}, f32[224,1000]{1,0:T(8,128)})) %all-reduce.9.cloned.1.call-update) | async-done | bytes 1792016 | tf_op jit(solution)/shard_map/psum | solution.py:92
  110.5 2.2 fusion.85
  113.2 1.0 copy-done.1
  114.9 3.6 collective-permute-start
  118.6 1.4 convolution_bitcast_fusion.5
  119.9 5.6 collective-permute-done
  125.5 2.0 fusion.78
  127.6 89.8 %all-reduce.7.cloned.1.call-done = (f32[224,224]{1,0:T(8,128)}, f32[224,224]{1,0:T(8,128)}) async-done(((f32[224,224]{1,0:T(8,128)}, f32[224,224]{1,0:T(8,128)}), (f32[224,224]{1,0:T(8,128)}, f32[224,224]{1,0:T(8,128)})) %all-reduce.7.cloned.1.call-update) | async-done | bytes 401424 | tf_op jit(solution)/shard_map/psum | solution.py:107
  217.4 29.3 %all-reduce.11.cloned.1.call-done = (f32[224,224]{1,0:T(8,128)}, f32[224,224]{1,0:T(8,128)}) async-done(((f32[224,224]{1,0:T(8,128)}, f32[224,224]{1,0:T(8,128)}), (f32[224,224]{1,0:T(8,128)}, f32[224,224]{1,0:T(8,128)})) %all-reduce.11.cloned.1.call-update) | async-done | bytes 401424 | tf_op jit(solution)/shard_map/psum | solution.py:107
  246.7 1.1 broadcast_multiply_fusion.1
  247.9 428.9 %while.180 = (s32[]{:T(128)}, f32[224,224]{1,0:T(8,128)S(1)}, f32[224,224]{0,1:T(8,128)S(1)}, s32[]{:T(128)}, s32[]{:T(128)}) while((s32[]{:T(128)}, f32[224,224]{1,0:T(8,128)S(1)}, f32[224,224]{0,1:T(8,128)S(1)}, s32[]{:T(128)}, s32[]{:T(128)}) %tuple.370), condition=%wide.region_10.11_spmd.clone.clone, body=%wide.region_8.0_spmd.clone.clone.sunk | while | flops 754882 | bytes 1041836 | solution.py:44
  676.8 374.4 %while.173 = (s32[]{:T(128)}, f32[224,224]{1,0:T(8,128)S(1)}, f32[224,224]{1,0:T(8,128)S(1)}, f32[224,224]{1,0:T(8,128)S(1)}, s32[]{:T(128)}, /*index=5*/s32[]{:T(128)}) while((s32[]{:T(128)}, f32[224,224]{1,0:T(8,128)S(1)}, f32[224,224]{1,0:T(8,128)S(1)}, f32[224,224]{1,0:T(8,128)S(1)}, s32[]{:T(128)}, ...), condition=%wide.region_15.16_spmd.clone, body=%wide.region_13.15_spmd.clone.sunk | while | flops 603233 | bytes 211545 | solution.py:58
  1051.4 374.4 %while.174 = (s32[]{:T(128)}, f32[224,224]{1,0:T(8,128)S(1)}, f32[224,224]{1,0:T(8,128)S(1)}, f32[224,224]{1,0:T(8,128)S(1)}, s32[]{:T(128)}, /*index=5*/s32[]{:T(128)}) while((s32[]{:T(128)}, f32[224,224]{1,0:T(8,128)S(1)}, f32[224,224]{1,0:T(8,128)S(1)}, f32[224,224]{1,0:T(8,128)S(1)}, s32[]{:T(128)}, ...), condition=%wide.region_18.19_spmd.clone, body=%wide.region_16.18_spmd.clone.sunk | while | flops 603233 | bytes 211545 | solution.py:58
  1426.5 67.4 %while.181 = (s32[]{:T(128)}, f32[40,40]{1,0:T(8,128)S(1)}, f32[40,40]{0,1:T(8,128)S(1)}, s32[]{:T(128)}, s32[]{:T(128)}) while((s32[]{:T(128)}, f32[40,40]{1,0:T(8,128)S(1)}, f32[40,40]{0,1:T(8,128)S(1)}, s32[]{:T(128)}, s32[]{:T(128)}) %tuple.379), condition=%wide.region_21.22_spmd.clone.clone, body=%wide.region_19.21_spmd.clone.clone.sunk | while | flops 24402 | bytes 49456 | solution.py:44
  1493.8 63.8 %while.175 = (s32[]{:T(128)}, f32[40,224]{1,0:T(8,128)S(1)}, f32[40,224]{1,0:T(8,128)S(1)}, f32[40,40]{1,0:T(8,128)S(1)}, s32[]{:T(128)}, /*index=5*/s32[]{:T(128)}) while((s32[]{:T(128)}, f32[40,224]{1,0:T(8,128)S(1)}, f32[40,224]{1,0:T(8,128)S(1)}, f32[40,40]{1,0:T(8,128)S(1)}, s32[]{:T(128)}, /*index=5*/s32[]{:T(128)}) %tuple.419), condition=%wide.region_24.25_spmd.clone, body=%wide.region_22.24_spmd.clone.sunk | while | flops 108089 | bytes 49913 | solution.py:58
  1558.1 67.4 %while.182 = (s32[]{:T(128)}, f32[40,40]{1,0:T(8,128)S(1)}, f32[40,40]{0,1:T(8,128)S(1)}, s32[]{:T(128)}, s32[]{:T(128)}) while((s32[]{:T(128)}, f32[40,40]{1,0:T(8,128)S(1)}, f32[40,40]{0,1:T(8,128)S(1)}, s32[]{:T(128)}, s32[]{:T(128)}) %tuple.385), condition=%wide.region_27.28_spmd.clone.clone, body=%wide.region_25.27_spmd.clone.clone.sunk | while | flops 24402 | bytes 49456 | solution.py:44
  1559.8 0.8 select_reduce_fusion.12
  1561.5 0.8 select_reduce_fusion.12
  1563.1 0.8 select_reduce_fusion.12
  1564.8 0.8 select_reduce_fusion.12
  1566.5 0.8 select_reduce_fusion.12
  1568.2 0.8 select_reduce_fusion.12
  1569.9 0.8 select_reduce_fusion.12
  1571.6 0.8 select_reduce_fusion.12
  1573.2 0.8 select_reduce_fusion.12
  1574.9 0.8 select_reduce_fusion.12
  1576.6 0.8 select_reduce_fusion.12
  1578.3 0.8 select_reduce_fusion.12
  1580.0 0.8 select_reduce_fusion.12
  1581.7 0.8 select_reduce_fusion.12
  1583.3 0.8 select_reduce_fusion.12
  1585.0 0.8 select_reduce_fusion.12
  1586.7 0.8 select_reduce_fusion.12
  1588.4 0.8 select_reduce_fusion.12
  1590.1 0.8 select_reduce_fusion.12
  1591.8 0.8 select_reduce_fusion.12
  1593.5 0.8 select_reduce_fusion.12
  1601.9 0.8 select_reduce_fusion.12
  1605.2 0.8 select_reduce_fusion.12
  1625.5 63.8 %while.176 = (s32[]{:T(128)}, f32[40,224]{1,0:T(8,128)S(1)}, f32[40,224]{1,0:T(8,128)S(1)}, f32[40,40]{1,0:T(8,128)S(1)}, s32[]{:T(128)}, /*index=5*/s32[]{:T(128)}) while((s32[]{:T(128)}, f32[40,224]{1,0:T(8,128)S(1)}, f32[40,224]{1,0:T(8,128)S(1)}, f32[40,40]{1,0:T(8,128)S(1)}, s32[]{:T(128)}, /*index=5*/s32[]{:T(128)}) %tuple.417), condition=%wide.region_30.31_spmd.clone, body=%wide.region_28.30_spmd.clone.sunk | while | flops 108089 | bytes 49913 | solution.py:58
  1689.7 67.3 %while.183 = (s32[]{:T(128)}, f32[40,40]{1,0:T(8,128)S(1)}, f32[40,40]{0,1:T(8,128)S(1)}, s32[]{:T(128)}, s32[]{:T(128)}) while((s32[]{:T(128)}, f32[40,40]{1,0:T(8,128)S(1)}, f32[40,40]{0,1:T(8,128)S(1)}, s32[]{:T(128)}, s32[]{:T(128)}) %tuple.391), condition=%wide.region_33.34_spmd.clone.clone, body=%wide.region_31.33_spmd.clone.clone.sunk | while | flops 24402 | bytes 49456 | solution.py:44
  1757.0 63.8 %while.177 = (s32[]{:T(128)}, f32[40,224]{1,0:T(8,128)S(1)}, f32[40,224]{1,0:T(8,128)S(1)}, f32[40,40]{1,0:T(8,128)S(1)}, s32[]{:T(128)}, /*index=5*/s32[]{:T(128)}) while((s32[]{:T(128)}, f32[40,224]{1,0:T(8,128)S(1)}, f32[40,224]{1,0:T(8,128)S(1)}, f32[40,40]{1,0:T(8,128)S(1)}, s32[]{:T(128)}, /*index=5*/s32[]{:T(128)}) %tuple.418), condition=%wide.region_36.37_spmd.clone, body=%wide.region_34.36_spmd.clone.sunk | while | flops 108089 | bytes 49913 | solution.py:58
  1821.3 67.3 %while.184 = (s32[]{:T(128)}, f32[40,40]{1,0:T(8,128)S(1)}, f32[40,40]{0,1:T(8,128)S(1)}, s32[]{:T(128)}, s32[]{:T(128)}) while((s32[]{:T(128)}, f32[40,40]{1,0:T(8,128)S(1)}, f32[40,40]{0,1:T(8,128)S(1)}, s32[]{:T(128)}, s32[]{:T(128)}) %tuple.397), condition=%wide.region_39.40_spmd.clone.clone, body=%wide.region_37.39_spmd.clone.clone.sunk | while | flops 24402 | bytes 49456 | solution.py:44
  1888.6 63.8 %while.178 = (s32[]{:T(128)}, f32[40,224]{1,0:T(8,128)S(1)}, f32[40,224]{1,0:T(8,128)S(1)}, f32[40,40]{1,0:T(8,128)S(1)}, s32[]{:T(128)}, /*index=5*/s32[]{:T(128)}) while((s32[]{:T(128)}, f32[40,224]{1,0:T(8,128)S(1)}, f32[40,224]{1,0:T(8,128)S(1)}, f32[40,40]{1,0:T(8,128)S(1)}, s32[]{:T(128)}, /*index=5*/s32[]{:T(128)}) %tuple.416), condition=%wide.region_42.43_spmd.clone, body=%wide.region_40.42_spmd.clone.sunk | while | flops 108089 | bytes 49913 | solution.py:58
  1954.1 336.9 %while.179 = (s32[]{:T(128)}, f32[224,40]{1,0:T(8,128)S(1)}, f32[224,40]{1,0:T(8,128)S(1)}, f32[224,224]{1,0:T(8,128)S(1)}, s32[]{:T(128)}, /*index=5*/s32[]{:T(128)}) while((s32[]{:T(128)}, f32[224,40]{1,0:T(8,128)S(1)}, f32[224,40]{1,0:T(8,128)S(1)}, f32[224,224]{1,0:T(8,128)S(1)}, s32[]{:T(128)}, /*index=5*/s32[]{:T(128)}) %tuple.403), condition=%wide.region_45.46_spmd.clone, body=%wide.region_43.45_spmd.clone.sunk | while | flops 108273 | bytes 121013 | solution.py:58
  2291.7 2.1 fusion.77
  (6335 shorter events, 1700.4 us)
Async XLA Ops:
  7.2 3.0 copy-start
  7.2 103.3 %all-reduce.9.cloned.1.call-start = ((), (), s32[]{:S(2)}) async-start(), calls=%async_computation.1 | async-start | bytes 3670016 | tf_op jit(solution)/shard_map/psum | solution.py:92
  11.5 205.8 %all-reduce.7.cloned.1.call-start = ((), (), s32[]{:S(2)}) async-start(), calls=%async_computation | async-start | bytes 917504 | tf_op jit(solution)/shard_map/psum | solution.py:107
  110.5 2.3 copy-start.2
  110.5 2.3 copy-start.3
  112.8 1.5 copy-start.1
  114.9 10.6 collective-permute-start
  127.5 119.2 %all-reduce.11.cloned.1.call-start = ((), (), s32[]{:S(2)}) async-start(), calls=%async_computation.2 | async-start | bytes 917504 | tf_op jit(solution)/shard_map/psum | solution.py:107
  2291.7 2.1 copy-start.4
Sparse Core Ops, SparseCore 0:
  12.1 98.3 all-reduce.8
  127.6 89.6 all-reduce.6
  219.7 26.9 all-reduce.10
